TPU v7x, 128 devices: a whole 4x4x4 slice. The times are simulated.
128 devices in a mesh: gx: 8 (over z, core), gy: 16 (over x, y).
Axes of the slice: x: 4, y: 4, z: 4, core: 2. Of those that a mesh axis runs over, the one named last changes fastest.
Arguments:
- tokens: bfloat16 [4096, 4096], P(('gx', 'gy')), may hold values from -3 to 3
- attn_gain: bfloat16 [4096], replicated, may hold values from 0.099609375 to 1.8984375
- mlp_gain: bfloat16 [4096], replicated, may hold values from 0.099609375 to 1.8984375
- w_query: bfloat16 [4096, 4096], P('gx', 'gy'), may hold values from -1 to 1
- w_key: bfloat16 [4096, 1024], P('gx', 'gy'), may hold values from -1 to 1
- value_projection: bfloat16 [4096, 1024], P('gx', 'gy'), may hold values from -0.09375 to 0.09375
- w_out: bfloat16 [4096, 4096], P('gy', 'gx'), may hold values from -0.09375 to 0.09375
- w_gate: bfloat16 [4096, 14336], P('gx', 'gy'), may hold values from -0.09375 to 0.09375
- w_up: bfloat16 [4096, 14336], P('gx', 'gy'), may hold values from -0.09375 to 0.09375
- w_down: bfloat16 [14336, 4096], P('gy', 'gx'), may hold values from -0.046875 to 0.046875
- lengths: int32 [6], replicated, may hold values from 1 to 3072, 4096 in all
- page_table: int32 [128, 2], replicated, may hold values from 0 to 15, as said below
Outputs:
- layer_out: bfloat16 [4096, 4096], P(('gx', 'gy'))
- paged_key_value_cache: bfloat16 [128, 2, 32, 1024], P('gx', None, None, 'gy')
Inputs may be any that keep to these rules, and one draw needn't show every extreme that they name: `page_table`: page p belongs to token group p // 16, the tokens of one index of gx. Its owner is an index of gx and its slot is below 16; every pair of owner and slot is taken by exactly one page. Of one token group's pages, 8 owners receive exactly 2 each and the other owners none.
All inputs are finite; a program needn't handle non-finite values.
Results may differ from a plain program's by a relative error of at most 0.025.
The roundings to bfloat16 on the way count: a program that leaves them out, or rounds other values in their place, can miss the bound.
Values may be sent and summed in bfloat16 or wider, within the bound.
A program may use at most 128 MiB of HBM per device.

v0:
```python
import jax
import jax.numpy as jnp
from jax import lax
from jax.sharding import PartitionSpec as P

HEAD_WIDTH = 128
WIN = 4096
PAGE_TOKENS = 32


rope_base = 10000.0
norm_eps = 1e-05
masked_score = -1e30


def partner(value, axis, distance):
    mask = 2**distance
    pairs = [(source, source ^ mask) for source in range(lax.axis_size(axis))]
    return lax.ppermute(value, axis, pairs)


def rms_scale(values, gain):
    floats = values.astype(jnp.float32)
    mean_square = jnp.mean(floats * floats, axis=-1, keepdims=True)
    return floats * lax.rsqrt(mean_square + norm_eps) * gain.astype(jnp.float32)


def segment_info(lengths, token_index):
    ends = jnp.cumsum(lengths, dtype=jnp.int32)
    starts = ends - lengths
    inside = (token_index[:, None] >= starts[None, :]).astype(jnp.int32)
    segment = jnp.sum(inside, axis=1, dtype=jnp.int32) - 1
    chosen = (segment[:, None] == jnp.arange(lengths.shape[0], dtype=jnp.int32)[None, :]).astype(
        jnp.int32
    )
    token_positions = token_index - jnp.sum(chosen * starts[None, :], axis=1, dtype=jnp.int32)
    return (segment, token_positions)


def apply_rotary(values, token_positions):
    half = values.shape[-1] // 2
    freq = rope_base ** (-jnp.arange(half, dtype=jnp.float32) * 2.0 / values.shape[-1])
    angle = token_positions.astype(jnp.float32)[:, None] * freq[None, :]
    cosine = jnp.cos(angle)[:, None, :]
    sine = jnp.sin(angle)[:, None, :]
    first = values[..., :half]
    second = values[..., half:]
    return jnp.concatenate(
        [first * cosine - second * sine, second * cosine + first * sine], axis=-1
    )


def join_halves(mine, other, lower):
    return jnp.where(
        lower, jnp.concatenate([mine, other], axis=1), jnp.concatenate([other, mine], axis=1)
    )


def row_products(source, pieces):
    return tuple((jnp.dot(source, piece, preferred_element_type=jnp.float32) for piece in pieces))


def per_device(
    tokens,
    attn_gain,
    mlp_gain,
    w_query,
    w_key,
    value_projection,
    w_out,
    w_gate,
    w_up,
    w_down,
    lengths,
    page_table,
):
    group_count = lax.axis_size("gx")
    local_rows = tokens.shape[0]
    group = local_rows * lax.axis_size("gy")
    group_index = lax.axis_index("gx")
    head_index = lax.axis_index("gy")
    group_start = group_index * group
    lower = head_index % 2 == 0
    query_cols = w_query.shape[1]
    query_heads = query_cols // HEAD_WIDTH
    key_cols = w_key.shape[1]
    key_heads = max(1, key_cols // HEAD_WIDTH)
    per_key = query_heads // key_heads
    normed = lax.all_gather(
        rms_scale(tokens, attn_gain).astype(jnp.bfloat16), "gy", axis=0, tiled=True
    )
    query = row_products(normed, (lax.all_gather(w_query, "gx", axis=0, tiled=True),))[0]
    key_weight, value_weight = (w_key, value_projection)
    unrotated_key, value_raw = row_products(
        normed,
        (
            lax.all_gather(key_weight, "gx", axis=0, tiled=True),
            lax.all_gather(value_weight, "gx", axis=0, tiled=True),
        ),
    )
    other_key, other_value = (
        partner(unrotated_key.astype(jnp.bfloat16), "gy", 0).astype(unrotated_key.dtype),
        partner(value_raw.astype(jnp.bfloat16), "gy", 0).astype(value_raw.dtype),
    )
    unrotated_key = join_halves(unrotated_key, other_key, lower)
    value_raw = join_halves(value_raw, other_value, lower)
    token_index = group_start + jnp.arange(group, dtype=jnp.int32)
    segment, token_positions = segment_info(lengths, token_index)
    query_rot = (
        apply_rotary(query.reshape(group, query_heads, HEAD_WIDTH), token_positions)
        .astype(jnp.bfloat16)
        .reshape(group, key_heads, per_key, HEAD_WIDTH)
    )
    rotated_key = (
        apply_rotary(unrotated_key.reshape(group, key_heads, HEAD_WIDTH), token_positions)
        .astype(jnp.bfloat16)
        .reshape(group, key_heads * HEAD_WIDTH)
    )
    value_vectors = value_raw.astype(jnp.bfloat16)
    scale = HEAD_WIDTH ** (-0.5)
    start_state = (
        jnp.full((key_heads, per_key, group), masked_score, jnp.float32),
        jnp.zeros((key_heads, per_key, group), jnp.float32),
        jnp.zeros((key_heads, per_key, group, HEAD_WIDTH), jnp.float32),
    )
    keys = lax.all_gather(rotated_key, "gx", axis=0, tiled=True)
    values = lax.all_gather(value_vectors, "gx", axis=0, tiled=True)
    count = keys.shape[0]
    key_index = jnp.arange(count, dtype=jnp.int32)
    key_segment, unused = segment_info(lengths, key_index)
    distance = token_index[:, None] - key_index[None, :]
    allowed = (segment[:, None] == key_segment[None, :]) & (distance >= 0) & (distance < WIN)

    def update(state):
        running, total, weighted = state
        scores = (
            jnp.einsum(
                "qhgd,khd->hgqk",
                query_rot,
                keys.reshape(count, key_heads, HEAD_WIDTH),
                preferred_element_type=jnp.float32,
            )
            * scale
        )
        masked = jnp.where(allowed[None, None], scores, masked_score)
        newest = jnp.maximum(running, jnp.max(masked, axis=-1))
        weights = jnp.where(allowed[None, None], jnp.exp(masked - newest[..., None]), 0.0)
        mixed = jnp.einsum(
            "hgqk,khd->hgqd",
            weights.astype(jnp.bfloat16),
            values.reshape(count, key_heads, HEAD_WIDTH),
            preferred_element_type=jnp.float32,
        )
        return (newest, jnp.sum(weights, axis=-1), mixed)

    state = lax.cond(jnp.any(allowed), update, lambda state: state, start_state)
    attended = (state[2] / state[1][..., None]).astype(jnp.bfloat16)
    attended = attended.transpose(2, 0, 1, 3).reshape(group, query_cols)
    partial_value = jnp.dot(
        attended,
        lax.all_gather(w_out, "gx", axis=1, tiled=True),
        preferred_element_type=jnp.float32,
    )
    share = lax.psum_scatter(
        partial_value.astype(jnp.bfloat16), "gy", scatter_dimension=0, tiled=True
    ).astype(jnp.float32)
    residual = (tokens.astype(jnp.float32) + share).astype(jnp.bfloat16)
    mlp_input = lax.all_gather(
        rms_scale(residual, mlp_gain).astype(jnp.bfloat16), "gy", axis=0, tiled=True
    )
    gate, up_values = row_products(
        mlp_input,
        (
            lax.all_gather(w_gate, "gx", axis=0, tiled=True),
            lax.all_gather(w_up, "gx", axis=0, tiled=True),
        ),
    )
    hidden = (jax.nn.silu(gate) * up_values).astype(jnp.bfloat16)
    down_full = lax.all_gather(w_down, "gx", axis=1, tiled=True)
    mlp_share = lax.psum_scatter(
        jnp.dot(hidden, down_full, preferred_element_type=jnp.float32).astype(jnp.bfloat16),
        "gy",
        scatter_dimension=0,
        tiled=True,
    ).astype(jnp.float32)
    layer_out = (residual.astype(jnp.float32) + mlp_share).astype(jnp.bfloat16)
    own_start = jnp.where(lower, 0, key_cols).astype(jnp.int32)
    local_key = lax.dynamic_slice_in_dim(rotated_key, own_start, key_cols, 1)
    own_value = lax.dynamic_slice_in_dim(value_vectors, own_start, key_cols, 1)
    slots_group = group // PAGE_TOKENS
    capacity = max(2, slots_group // group_count)
    pages_local = (
        jnp.stack([local_key, own_value], axis=0)
        .reshape(2, slots_group, PAGE_TOKENS, key_cols)
        .transpose(1, 0, 2, 3)
        .reshape(slots_group, 2 * PAGE_TOKENS * key_cols)
    )
    owner = page_table[:, 0]
    slot = page_table[:, 1]
    page_index = jnp.arange(owner.shape[0], dtype=jnp.int32)
    page_group = page_index // slots_group
    before = (
        (page_group[:, None] == page_group[None, :])
        & (owner[:, None] == owner[None, :])
        & (page_index[None, :] < page_index[:, None])
    )
    rank = jnp.sum(before.astype(jnp.int32), axis=1, dtype=jnp.int32)
    my_owner = lax.dynamic_slice_in_dim(owner, group_index * slots_group, slots_group, 0)
    my_rank = lax.dynamic_slice_in_dim(rank, group_index * slots_group, slots_group, 0)
    target = jnp.arange(group_count * capacity, dtype=jnp.int32)
    select = (
        (my_owner[None, :] == target[:, None] // capacity)
        & (my_rank[None, :] == target[:, None] % capacity)
    ).astype(jnp.bfloat16)
    outgoing = (
        jnp.dot(select, pages_local, preferred_element_type=jnp.float32)
        .astype(jnp.bfloat16)
        .reshape(group_count, capacity, 2, PAGE_TOKENS, key_cols)
    )
    incoming = lax.all_to_all(outgoing, "gx", split_axis=0, concat_axis=0, tiled=True)
    column = page_group * capacity + rank
    pick = (
        (owner[None, :] == group_index)
        & (slot[None, :] == jnp.arange(slots_group, dtype=jnp.int32)[:, None])
    ).astype(jnp.float32)
    place = (column[:, None] == target[None, :]).astype(jnp.float32)
    routing = jnp.dot(pick, place, preferred_element_type=jnp.float32).astype(jnp.bfloat16)
    paged_key_value_cache = (
        jnp.dot(
            routing,
            incoming.reshape(group_count * capacity, 2 * PAGE_TOKENS * key_cols),
            preferred_element_type=jnp.float32,
        )
        .astype(jnp.bfloat16)
        .reshape(slots_group, 2, PAGE_TOKENS, key_cols)
    )
    return (layer_out, paged_key_value_cache)


def solution(mesh):
    placed = (
        P(("gx", "gy"), None),
        P(),
        P(),
        P("gx", "gy"),
        P("gx", "gy"),
        P("gx", "gy"),
        P("gy", "gx"),
        P("gx", "gy"),
        P("gx", "gy"),
        P("gy", "gx"),
        P(),
        P(),
    )
    return jax.shard_map(
        per_device,
        mesh=mesh,
        in_specs=placed,
        out_specs=(P(("gx", "gy"), None), P("gx", None, None, "gy")),
        check_vma=False,
    )
```

profile of v0, /device:TPU:0, one launch (start us, length us, event | category | flops | bytes accessed | tf_op | source)
XLA Modules:
  0.0 550.2 jit_solution(15981981439846609788)
XLA Ops:
  7.2 0.7 convert_element_type.115
  7.9 1.1 fusion.21
  9.1 1.8 fusion.23
  10.9 0.7 all-gather.12.cloned.1.call-update
  11.7 0.8 reduce-window.9
  12.5 0.7 bitcast_subtract_fusion
  13.4 14.6 %all_gather.35 = bf16[4096,64]{0,1:T(8,128)(2,1)S(1)} all-gather(bf16[512,64]{0,1:T(8,128)(2,1)} %param.18), channel_id=1, replica_groups=mesh['gx'=8,'gy'=16] {'gx'}, dimensions={0}, use_global_device_ids=true | all-gather | bytes 589824 | tf_op jit(solution)/shard_map/all_gather | solution.py:97
  28.0 36.9 %all-gather.10.cloned.1.call-done = bf16[512,4096]{1,0:T(8,128)(2,1)} async-done(((bf16[32,4096]{1,0:T(8,128)(2,1)}), bf16[512,4096]{1,0:T(8,128)(2,1)}) %all-gather.10.cloned.1.call-update) | async-done | bytes 4194320 | tf_op jit(solution)/shard_map/all_gather | solution.py:89
  64.9 3.6 fusion.62
  68.5 1.5 collective-permute-start
  70.0 2.8 collective-permute-done
  72.9 0.6 fusion.37
  73.4 0.7 pad_maximum_fusion.1
  74.2 14.2 %all_gather.37 = bf16[4096,64]{0,1:T(8,128)(2,1)S(1)} all-gather(bf16[512,64]{0,1:T(8,128)(2,1)S(1)} %copy-done.3), channel_id=1, replica_groups=mesh['gx'=8,'gy'=16] {'gx'}, dimensions={0}, use_global_device_ids=true | all-gather | bytes 589824 | tf_op jit(solution)/shard_map/all_gather | solution.py:98
  88.3 3.7 fusion.64
  92.0 1.8 collective-permute-start.1
  93.8 2.6 collective-permute-done.1
  96.4 0.7 fusion.31
  97.2 0.5 all-gather.18.cloned.1.call-update
  97.8 0.1 convert_reduce_fusion
  97.9 3.6 fusion.20
  102.1 1.8 multiply_cosine_fusion
  103.9 4.2 fusion.63
  108.1 0.2 copy.44
  108.3 0.2 copy.45
  108.5 1.2 fusion.29
  109.7 0.1 pad_maximum_fusion
  109.9 7.8 %all-gather.14.cloned.1.call-done = bf16[4096,128]{0,1:T(8,128)(2,1)} async-done(((bf16[512,128]{0,1:T(8,128)(2,1)}), bf16[4096,128]{0,1:T(8,128)(2,1)}) %all-gather.14.cloned.1.call-update) | async-done | bytes 1048592 | tf_op jit(solution)/shard_map/all_gather | solution.py:126
  117.7 25.0 %all-gather.16.cloned.1.call-done = bf16[4096,128]{0,1:T(8,128)(2,1)} async-done(((bf16[512,128]{0,1:T(8,128)(2,1)}), bf16[4096,128]{0,1:T(8,128)(2,1)}) %all-gather.16.cloned.1.call-update) | async-done | bytes 1048592 | tf_op jit(solution)/shard_map/all_gather | solution.py:127
  142.8 14.2 %conditional.1 = (f32[1,2,512]{2,1,0:T(2,128)S(1)}, f32[1,2,512,128]{2,3,1,0:T(8,128)S(1)}) conditional(s32[]{:T(128)} %convert_element_type.114, () %tuple.16, (pred[512,4096]{0,1:T(8,128)(4,1)S(1)}, bf16[512,1,2,128]{3,0,2,1:T(8,128)(2,1)S(1)}, bf16[4096,128]{0,1:T(8,128)(2,1)}, bf16[4096,128]{0,1:T(8,128)(2,1)}) %tuple.17), branch_computations={%region_6.7_spmd, %region_7.10_spmd} | conditional | flops 2202008576 | bytes 63725612 | solution.py:156
  142.8 5.1 fusion
  147.9 4.6 fusion.7
  152.5 4.4 fusion.2
  157.0 12.6 %all-gather.18.cloned.1.call-done = bf16[256,4096]{1,0:T(8,128)(2,1)} async-done(((bf16[256,512]{1,0:T(8,128)(2,1)}), bf16[256,4096]{1,0:T(8,128)(2,1)}) %all-gather.18.cloned.1.call-update) | async-done | bytes 2097168 | tf_op jit(solution)/shard_map/all_gather | solution.py:161
  169.6 4.9 convolution_convert_fusion.1
  174.6 0.7 all-gather.22.cloned.1.call-update
  175.4 77.2 %reduce-scatter.3.cloned.1.call-done = bf16[32,4096]{1,0:T(8,128)(2,1)} async-done(((bf16[512,4096]{1,0:T(8,128)(2,1)}), bf16[32,4096]{1,0:T(8,128)(2,1)}) %reduce-scatter.3.cloned.1.call-update) | async-done | bytes 262160 | tf_op jit(solution)/shard_map/reduce_scatter | solution.py:164
  252.6 1.1 fusion.25
  253.7 1.8 fusion.27
  255.6 0.7 all-gather.24.cloned.1.call-update
  256.3 0.5 all-gather.26.cloned.1.call-update
  256.9 0.3 reduce-scatter.5.cloned.1.call-start
  257.1 42.2 %all-gather.22.cloned.1.call-done = bf16[4096,896]{1,0:T(8,128)(2,1)} async-done(((bf16[512,896]{1,0:T(8,128)(2,1)}), bf16[4096,896]{1,0:T(8,128)(2,1)}) %all-gather.22.cloned.1.call-update) | async-done | bytes 7340048 | tf_op jit(solution)/shard_map/all_gather | solution.py:174
  299.4 54.3 %all-gather.20.cloned.1.call-done = bf16[512,4096]{1,0:T(8,128)(2,1)} async-done(((bf16[32,4096]{1,0:T(8,128)(2,1)}), bf16[512,4096]{1,0:T(8,128)(2,1)}) %all-gather.20.cloned.1.call-update) | async-done | bytes 4194320 | tf_op jit(solution)/shard_map/all_gather | solution.py:168
  353.7 9.8 %fusion.65 = f32[512,896]{1,0:T(8,128)S(1)} fusion(bf16[512,4096]{1,0:T(8,128)(2,1)} %all-gather.20.cloned.1.call-done, bf16[4096,896]{1,0:T(8,128)(2,1)} %all-gather.22.cloned.1.call-done), kind=kOutput, calls=%fused_computation.120 | convolution fusion | flops 3758096384 | bytes 13369344 | tf_op jit(solution)/shard_map/dot_general | solution.py:60
  363.5 37.2 %all-gather.24.cloned.1.call-done = bf16[4096,896]{1,0:T(8,128)(2,1)} async-done(((bf16[512,896]{1,0:T(8,128)(2,1)}), bf16[4096,896]{1,0:T(8,128)(2,1)}) %all-gather.24.cloned.1.call-update) | async-done | bytes 7340048 | tf_op jit(solution)/shard_map/all_gather | solution.py:175
  400.8 47.2 %all-gather.26.cloned.1.call-done = bf16[896,4096]{1,0:T(8,128)(2,1)} async-done(((bf16[896,512]{1,0:T(8,128)(2,1)}), bf16[896,4096]{1,0:T(8,128)(2,1)}) %all-gather.26.cloned.1.call-update) | async-done | bytes 7340048 | tf_op jit(solution)/shard_map/all_gather | solution.py:179
  448.0 16.3 %convolution_convert_fusion = bf16[512,4096]{1,0:T(8,128)(2,1)} fusion(bf16[896,4096]{1,0:T(8,128)(2,1)} %all-gather.26.cloned.1.call-done, f32[512,896]{1,0:T(8,128)S(1)} %fusion.65, bf16[512,4096]{1,0:T(8,128)(2,1)} %all-gather.20.cloned.1.call-done, bf16[4096,896]{1,0:T(8,128)(2,1)} %all-gather.24.cloned.1.call-done), kind=kOutput, calls=%fused_computation.22 | convolution fusion | flops 7521042432 | bytes 24903680 | tf_op jit(solution)/shard_map/dot_general | solution.py:181
  464.3 0.6 copy-done.5
  464.9 0.2 convert_reduce_fusion.1
  465.3 0.1 copy.34
  465.5 0.1 copy.35
  465.7 0.3 reshape.446
  466.0 0.2 convolution_convert_fusion.3
  466.2 0.2 reshape.447
  466.5 0.9 reshape.453
  467.4 3.4 all-to-all-start
  470.7 6.0 %all-to-all-done = bf16[8,2,4096]{2,1,0:T(2,128)(2,1)S(1)} async-done(((bf16[8,2,4096]{2,1,0:T(2,128)(2,1)}), bf16[8,2,4096]{2,1,0:T(2,128)(2,1)S(1)}, u32[]{:S(2)}, u32[]{:S(2)}) %all-to-all-start) | async-done | bytes 131104 | tf_op jit(solution)/shard_map/all_to_all | solution.py:220
  476.8 0.2 reshape.454
  477.0 0.3 reshape.448
  477.3 0.4 convolution_convert_fusion.2
  477.7 1.0 reshape.449
  478.6 63.3 %reduce-scatter.5.cloned.1.call-done = bf16[32,4096]{1,0:T(8,128)(2,1)} async-done(((bf16[512,4096]{1,0:T(8,128)(2,1)}), bf16[32,4096]{1,0:T(8,128)(2,1)}) %reduce-scatter.5.cloned.1.call-update) | async-done | bytes 262160 | tf_op jit(solution)/shard_map/reduce_scatter | solution.py:180
  541.9 1.7 fusion.28
  (56 shorter events, 1.2 us)
Async XLA Ops:
  7.2 57.7 %all-gather.10.cloned.1.call-start = ((), (), s32[]{:S(2)}) async-start(), calls=%async_computation.3 | async-start | bytes 4456448 | tf_op jit(solution)/shard_map/all_gather | solution.py:89
  7.9 66.3 %copy-start.3 = (bf16[512,64]{0,1:T(8,128)(2,1)S(1)}, bf16[512,64]{0,1:T(8,128)(2,1)}, u32[]{:S(2)}) copy-start(bf16[512,64]{0,1:T(8,128)(2,1)} %param.19) | copy-start | bytes 196612
  10.9 93.0 %all-gather.12.cloned.1.call-start = ((), (), s32[]{:S(2)}) async-start(), calls=%async_computation.4 | async-start | bytes 2359296 | tf_op jit(solution)/shard_map/all_gather | solution.py:92
  11.6 106.1 %all-gather.14.cloned.1.call-start = ((), (), s32[]{:S(2)}) async-start(), calls=%async_computation.5 | async-start | bytes 1179648 | tf_op jit(solution)/shard_map/all_gather | solution.py:126
  68.5 4.3 collective-permute-start
  74.1 68.7 %all-gather.16.cloned.1.call-start = ((), (), s32[]{:S(2)}) async-start(), calls=%async_computation.6 | async-start | bytes 1179648 | tf_op jit(solution)/shard_map/all_gather | solution.py:127
  92.0 4.4 collective-permute-start.1
  97.1 72.5 %all-gather.18.cloned.1.call-start = ((), (), s32[]{:S(2)}) async-start(), calls=%async_computation.7 | async-start | bytes 2359296 | tf_op jit(solution)/shard_map/all_gather | solution.py:161
  97.7 154.9 %reduce-scatter.3.cloned.1.call-start = ((), (), s32[]{:S(2)}) async-start(), calls=%async_computation.8 | async-start | bytes 4456448 | tf_op jit(solution)/shard_map/reduce_scatter | solution.py:164
  142.8 5.2 copy-start.6
  174.6 0.8 copy-start.4
  174.6 78.0 %copy-start = (bf16[32,4096]{1,0:T(8,128)(2,1)S(1)}, bf16[32,4096]{1,0:T(8,128)(2,1)}, u32[]{:S(2)}) copy-start(bf16[32,4096]{1,0:T(8,128)(2,1)} %param.14) | copy-start | bytes 786436
  174.6 124.8 %all-gather.22.cloned.1.call-start = ((), (), s32[]{:S(2)}) async-start(), calls=%async_computation.10 | async-start | bytes 8257536 | tf_op jit(solution)/shard_map/all_gather | solution.py:174
  175.3 178.4 %all-gather.20.cloned.1.call-start = ((), (), s32[]{:S(2)}) async-start(), calls=%async_computation.9 | async-start | bytes 4456448 | tf_op jit(solution)/shard_map/all_gather | solution.py:168
  255.5 145.2 %all-gather.24.cloned.1.call-start = ((), (), s32[]{:S(2)}) async-start(), calls=%async_computation.11 | async-start | bytes 8257536 | tf_op jit(solution)/shard_map/all_gather | solution.py:175
  256.3 191.7 %all-gather.26.cloned.1.call-start = ((), (), s32[]{:S(2)}) async-start(), calls=%async_computation.12 | async-start | bytes 8257536 | tf_op jit(solution)/shard_map/all_gather | solution.py:179
  256.9 285.0 %reduce-scatter.5.cloned.1.call-start = ((), (), s32[]{:S(2)}) async-start(), calls=%async_computation.13 | async-start | bytes 4456448 | tf_op jit(solution)/shard_map/reduce_scatter | solution.py:180
  464.2 0.7 copy-start.5
  464.2 1.2 copy-start.2
  464.2 77.7 %copy-start.1 = (bf16[32,4096]{1,0:T(8,128)(2,1)S(1)}, bf16[32,4096]{1,0:T(8,128)(2,1)}, u32[]{:S(2)}) copy-start(bf16[32,4096]{1,0:T(8,128)(2,1)} %reduce-scatter.3.cloned.1.call-done) | copy-start | bytes 786436
  467.4 9.4 %all-to-all-start = ((bf16[8,2,4096]{2,1,0:T(2,128)(2,1)}), bf16[8,2,4096]{2,1,0:T(2,128)(2,1)S(1)}, u32[]{:S(2)}, u32[]{:S(2)}) async-start(bf16[8,2,4096]{2,1,0:T(2,128)(2,1)} %reshape.453), calls=%async_computation.2 | async-start | bytes 262144 | tf_op jit(solution)/shard_map/all_to_all | solution.py:220
Sparse Core Ops, SparseCore 0:
  11.0 53.8 all-gather.9
  66.6 25.7 all-gather.11
  94.1 23.5 all-gather.13
  119.3 23.4 all-gather.15
  144.3 25.2 all-gather.17
  174.7 77.8 reduce-scatter.2
  254.4 44.9 all-gather.21
  302.3 51.3 all-gather.19
  355.5 45.2 all-gather.23
  402.4 45.4 all-gather.25
  464.4 77.4 reduce-scatter.4
where the time goes:
time: 551 us; the launch traced here: 550 us
  waiting for transfers between devices  419 us (76%)
  matrix products  52.7 us (10%)
  blocking collectives  28.8 us (5%)
  other arithmetic  23.6 us (4%)
  between operations  14.8 us (3%)
  starting transfers between devices  7.29 us (1%)
    reduce_scatter x1, waiting for transfers between devices, per_device(): lax.psum_scatter(partial_value.astype(jnp.bfloat16), 'gy', scatter_dimens...  77.2 us
    reduce_scatter x1, waiting for transfers between devices, per_device(): lax.psum_scatter(jnp.dot(hidden, down_full, preferred_element_type=jnp.fl...  63.3 us
    all_gather x1, waiting for transfers between devices, per_device(): lax.all_gather(rms_scale(residual, mlp_gain).astype(jnp.bfloat16), 'gy',...  54.3 us
    all_gather x1, waiting for transfers between devices, per_device(): down_full = lax.all_gather(w_down, 'gx', axis=1, tiled=True)  47.2 us
    all_gather x1, waiting for transfers between devices, per_device(): lax.all_gather(w_gate, 'gx', axis=0, tiled=True)  42.2 us
    all_gather x1, waiting for transfers between devices, per_device(): lax.all_gather(w_up, 'gx', axis=0, tiled=True)  37.2 us
    all_gather x1, waiting for transfers between devices, per_device(): lax.all_gather(rms_scale(tokens, attn_gain).astype(jnp.bfloat16), 'gy', a...  36.9 us
    all_gather x1, waiting for transfers between devices, per_device(): values = lax.all_gather(value_vectors, 'gx', axis=0, tiled=True)  25 us
  transfers between devices with their start and end apart: 14, of which 13 were waited for; matrix products, arithmetic and copies ran while one was open for 10% of the time, Pallas kernels for 0%

commit v1 on v0

v1 whole, which is shorter than its diff:
```python
import functools

import jax
import jax.numpy as jnp
from jax import lax
from jax.experimental import pallas as pl
from jax.experimental.pallas import tpu as pltpu
from jax.sharding import PartitionSpec as P

HEAD = 128
PAGE = 32
WIDTH = 4096
GROUP = 512
LOCAL = 32
HIDDEN = 896
HALF = WIDTH // 2
QUARTER = WIDTH // 4
ROPE_BASE = 10000.0
EPS = 1e-05
MASKED = -1e30
F32 = jnp.float32
BF16 = jnp.bfloat16
MESH = pl.DeviceIdType.MESH
VMEM_LIMIT = 66_000_000


def mod4(value):
    return lax.rem(value + 4, 4)


def dot(a, b):
    return jnp.dot(a, b, preferred_element_type=F32)


class Net:
    def __init__(self, send, recv):
        self.send, self.recv, self.used, self.started = send, recv, 0, []
        self.g, self.h = lax.axis_index("gx"), lax.axis_index("gy")
        self.z, self.c = lax.div(self.g, 2), lax.rem(self.g, 2)
        self.x, self.y = lax.div(self.h, 4), lax.rem(self.h, 4)

    def along_z(self, d):
        return (mod4(self.z + d) * 2 + self.c, self.h)

    def partner(self):
        return (self.z * 2 + 1 - self.c, self.h)

    def plane(self, dx, dy):
        return (self.g, mod4(self.x + dx) * 4 + mod4(self.y + dy))

    def barrier(self):
        peers = [self.along_z(1), self.along_z(-1), self.partner()]
        peers += [self.plane(1, 0), self.plane(-1, 0), self.plane(0, 1), self.plane(0, -1)]
        sem = pltpu.get_barrier_semaphore()
        for peer in peers:
            pl.semaphore_signal(sem, inc=1, device_id=peer, device_id_type=MESH)
        pl.semaphore_wait(sem, len(peers))

    def put(self, src, dst, to):
        index = self.used
        self.used += 1
        copy = pltpu.make_async_remote_copy(
            src_ref=src,
            dst_ref=dst,
            send_sem=self.send.at[index],
            recv_sem=self.recv.at[index],
            device_id=to,
            device_id_type=MESH,
        )
        copy.start()
        self.started.append(copy)
        return (index, to)

    def got(self, tag, dst):
        index, to = tag
        pltpu.make_async_remote_copy(
            src_ref=dst,
            dst_ref=dst,
            send_sem=self.send.at[index],
            recv_sem=self.recv.at[index],
            device_id=to,
            device_id_type=MESH,
        ).wait_recv()

    def finish(self):
        for copy in self.started:
            copy.wait_send()
        self.started = []


class PlaneGather:
    def __init__(self, net, buf):
        self.net, self.buf = net, buf
        self.first, self.relay1, self.second, self.relay2 = {}, {}, {}, {}

    def view(self, h, da, db, q=None):
        n = self.net
        a, b = (n.x, n.y) if h == 0 else (n.y, n.x)
        a, b = mod4(a + da), mod4(b + db)
        slot = a * 4 + b if h == 0 else b * 4 + a
        cols = pl.ds(h * HALF, HALF) if q is None else pl.ds(h * HALF + q * QUARTER, QUARTER)
        return self.buf.at[slot, :, cols]

    def to(self, h, da, db):
        return self.net.plane(da, db) if h == 0 else self.net.plane(db, da)

    def put(self, h, da, db, q, ta, tb):
        ref = self.view(h, da, db, q)
        return self.net.put(ref, ref, self.to(h, ta, tb))

    def start(self):
        for h in (0, 1):
            for d in (1, -1):
                self.first[h, d] = self.put(h, 0, 0, None, d, 0)
        for h in (0, 1):
            for d in (1, -1):
                self.second[h, 0, d] = self.put(h, 0, 0, None, 0, d)

    def step1(self):
        for d in (1, -1):
            for h in (0, 1):
                self.net.got(self.first[h, d], self.view(h, -d, 0))
                self.relay1[h, d] = self.put(h, -d, 0, 0 if d == 1 else 1, d, 0)
                for e in (1, -1):
                    self.second[h, -d, e] = self.put(h, -d, 0, None, 0, e)

    def pass_on(self, j):
        for d in (1, -1):
            for h in (0, 1):
                self.net.got(self.second[h, j, d], self.view(h, j, -d))
                self.relay2[h, j, d] = self.put(h, j, -d, 0 if d == 1 else 1, 0, d)

    def step2(self):
        self.pass_on(0)

    def step3(self):
        for h in (0, 1):
            for d in (1, -1):
                self.net.got(self.relay1[h, d], self.view(h, 2, 0, 0 if d == 1 else 1))
            for e in (1, -1):
                self.second[h, 2, e] = self.put(h, 2, 0, None, 0, e)

    def step4(self):
        self.pass_on(-1)
        self.pass_on(1)

    def step5(self):
        self.pass_on(2)

    def step6(self):
        for j in (0, -1, 1, 2):
            for h in (0, 1):
                for d in (1, -1):
                    self.net.got(self.relay2[h, j, d], self.view(h, j, 2, 0 if d == 1 else 1))


class PlaneScatter:
    def __init__(self, net, part, near, far, total, small):
        self.net, self.part, self.total = net, part, total
        self.r1, self.ri, self.r2 = near, far, None
        self.near, self.small = near, small
        self.tags = {}

    def pos(self, h):
        n = self.net
        return (n.x, n.y) if h == 0 else (n.y, n.x)

    def to(self, h, ta, tb):
        return self.net.plane(ta, tb) if h == 0 else self.net.plane(tb, ta)

    def chunk(self, h, q, da):
        at = mod4(self.pos(h)[0] + da)
        cols = pl.ds(h * HALF + q * QUARTER, QUARTER)
        if h == 0:
            return self.part.at[at, :, :, cols]
        return self.part.at[:, at, :, cols]

    def row(self, h, q, db):
        return self.total.at[h * 2 + q, mod4(self.pos(h)[1] + db)]

    def step1(self, h, q):
        d = 1 if q == 0 else -1
        k = h * 2 + q
        self.tags[k, 0] = self.net.put(self.chunk(h, q, 2), self.near.at[k, 0], self.to(h, d, 0))
        self.tags[k, 1] = self.net.put(self.chunk(h, q, -d), self.near.at[k, 1], self.to(h, -d, 0))

    def step2(self, h, q):
        d = 1 if q == 0 else -1
        k = h * 2 + q
        self.net.got(self.tags[k, 0], self.near.at[k, 0])
        mine = self.chunk(h, q, d)
        mine[...] = (mine[...].astype(F32) + self.near[k, 0].astype(F32)).astype(BF16)
        self.tags[k, 2] = self.net.put(mine, self.near.at[k, 2], self.to(h, d, 0))

    def step3(self, h, q):
        d = 1 if q == 0 else -1
        k = h * 2 + q
        self.net.got(self.tags[k, 1], self.near.at[k, 1])
        self.net.got(self.tags[k, 2], self.near.at[k, 2])
        mine = self.chunk(h, q, 0)
        self.total[k] = (
            mine[...].astype(F32) + self.near[k, 1].astype(F32) + self.near[k, 2].astype(F32)
        ).astype(BF16)
        self.tags[k, 3] = self.net.put(self.row(h, q, 2), self.small.at[k, 0], self.to(h, 0, d))
        self.tags[k, 4] = self.net.put(self.row(h, q, -d), self.small.at[k, 1], self.to(h, 0, -d))

    def step4(self, h, q):
        d = 1 if q == 0 else -1
        k = h * 2 + q
        self.net.got(self.tags[k, 3], self.small.at[k, 0])
        mine = self.row(h, q, d)
        mine[...] = (mine[...].astype(F32) + self.small[k, 0].astype(F32)).astype(BF16)
        self.tags[k, 5] = self.net.put(mine, self.small.at[k, 2], self.to(h, 0, d))

    def step5(self, h, q):
        k = h * 2 + q
        self.net.got(self.tags[k, 4], self.small.at[k, 1])
        self.net.got(self.tags[k, 5], self.small.at[k, 2])
        mine = self.row(h, q, 0)
        return mine[...].astype(F32) + self.small[k, 1].astype(F32) + self.small[k, 2].astype(F32)


QUARTERS = ((0, 0), (1, 0), (0, 1), (1, 1))


class ColumnGather:
    def __init__(self, net, src, slot, sem, rows):
        self.net, self.src, self.slot, self.sem, self.rows = net, src, slot, sem, rows
        self.zs, self.relays, self.fwd, self.fwdr = {}, {}, {}, {}

    def at(self, dz, other=False, half=None):
        n = self.net
        core = 1 - n.c if other else n.c
        return self.slot(mod4(n.z + dz) * 2 + core, half)

    def start(self):
        n = self.net
        for d in (1, -1):
            self.zs[d] = n.put(self.src, self.at(0), n.along_z(d))

    def start_local(self):
        self.pair = self.net.put(self.src, self.at(0), self.net.partner())
        self.own = pltpu.make_async_copy(self.src, self.at(0), self.sem)
        self.own.start()

    def relay(self):
        n = self.net
        for d in (1, -1):
            n.got(self.zs[d], self.at(-d))
            part = self.at(-d, half=0 if d == 1 else 1)
            self.relays[d] = n.put(part, part, n.along_z(d))
            self.fwd[d] = n.put(self.at(-d), self.at(-d), n.partner())

    def forward(self):
        n = self.net
        for d in (1, -1):
            part = self.at(2, half=0 if d == 1 else 1)
            n.got(self.relays[d], part)
            self.fwdr[d] = n.put(part, part, n.partner())

    def wait(self):
        n = self.net
        self.own.wait()
        n.got(self.pair, self.at(0, True))
        for d in (1, -1):
            n.got(self.fwd[d], self.at(-d, True))
        for d in (1, -1):
            n.got(self.fwdr[d], self.at(2, True, 0 if d == 1 else 1))


def half_rows(buf, rows):
    def slot(index, half):
        if half is None:
            return buf.at[index]
        return buf.at[index, pl.ds(half * (rows // 2), rows // 2)]

    return slot


def rms(values, gain):
    mean_square = jnp.mean(values * values, axis=-1, keepdims=True)
    return values * lax.rsqrt(mean_square + EPS) * gain


def front_kernel(
    tokens, gain, cos, sin, wqkv, q_out, kv_out,
    x_all, w_all, pair_src, pair_all, send, recv, own_sem,
):
    net = Net(send, recv)
    net.barrier()
    weights = ColumnGather(net, wqkv, half_rows(w_all, GROUP), own_sem.at[0], GROUP)
    weights.start()
    lower = lax.rem(net.y, 2) == 0
    other = (net.g, net.x * 4 + net.y + 1 - 2 * lax.rem(net.y, 2))
    swap = net.put(wqkv.at[:, pl.ds(2 * HEAD, HEAD)], pair_src, other)
    weights.start_local()
    values = tokens[...].astype(F32)
    x_all[net.h] = rms(values, gain[...].astype(F32)).astype(BF16)
    gather = PlaneGather(net, x_all)
    gather.start()
    pairs = ColumnGather(net, pair_src, half_rows(pair_all, GROUP), own_sem.at[1], GROUP)
    net.got(swap, pair_src)
    pairs.start()
    pairs.start_local()
    gather.step1()
    gather.step2()
    weights.relay()
    gather.step3()
    pairs.relay()
    gather.step4()
    weights.forward()
    pairs.forward()
    gather.step5()
    weights.wait()
    pairs.wait()
    gather.step6()

    lane = lax.broadcasted_iota(jnp.int32, (256, HEAD), 1)
    low = lane < HEAD // 2

    @pl.loop(0, 2)
    def _(r):
        main = jnp.zeros((256, 3 * HEAD), F32)
        side = jnp.zeros((256, HEAD), F32)
        for k in range(8):
            rows = x_all[pl.ds(r * 8, 8), :, k * GROUP:(k + 1) * GROUP].reshape(256, GROUP)
            main = main + dot(rows, w_all[k])
            side = side + dot(rows, pair_all[k])
        c = cos[pl.ds(r * 256, 256), :]
        s = sin[pl.ds(r * 256, 256), :]

        def rotate(v):
            return (v * c + pltpu.roll(v, HEAD // 2, 1) * s).astype(BF16)

        mine = main[:, 2 * HEAD:]
        even = jnp.where(lower, mine, side)
        odd = jnp.where(lower, side, mine)
        key = jnp.where(low, even, pltpu.roll(odd, HEAD // 2, 1))
        value = jnp.where(low, pltpu.roll(even, HEAD // 2, 1), odd)
        at = pl.ds(r * 256, 256)
        q_out[at, 0:HEAD] = rotate(main[:, 0:HEAD])
        q_out[at, HEAD:2 * HEAD] = rotate(main[:, HEAD:2 * HEAD])
        kv_out[pl.ds(r * 8, 8), :, 0:HEAD] = rotate(key).reshape(8, PAGE, HEAD)
        kv_out[pl.ds(r * 8, 8), :, HEAD:2 * HEAD] = value.astype(BF16).reshape(8, PAGE, HEAD)

    net.finish()


def vmem():
    return pl.BlockSpec(memory_space=pltpu.VMEM)


def anywhere():
    return pl.BlockSpec(memory_space=pl.ANY)


def front(tokens, gain, cos, sin, wqkv):
    return pl.pallas_call(
        front_kernel,
        out_shape=(
            jax.ShapeDtypeStruct((GROUP, 2 * HEAD), BF16),
            jax.ShapeDtypeStruct((16, PAGE, 2 * HEAD), BF16),
        ),
        in_specs=[vmem()] * 4 + [anywhere()],
        out_specs=(vmem(), vmem()),
        scratch_shapes=[
            pltpu.VMEM((16, LOCAL, WIDTH), BF16),
            pltpu.VMEM((8, GROUP, 3 * HEAD), BF16),
            pltpu.VMEM((GROUP, HEAD), BF16),
            pltpu.VMEM((8, GROUP, HEAD), BF16),
            pltpu.SemaphoreType.DMA((64,)),
            pltpu.SemaphoreType.DMA((64,)),
            pltpu.SemaphoreType.DMA((2,)),
        ],
        compiler_params=pltpu.CompilerParams(
            collective_id=0, has_side_effects=True, vmem_limit_bytes=VMEM_LIMIT
        ),
        name="front",
    )(tokens, gain, cos, sin, wqkv)


def back_kernel(
    inv, q, kv, begin, tokens, gain, wo, wg, wu, wd, out, cache,
    kv_all, wo_all, wg_all, wu_all, wd_all, x_all, part, near, total, small,
    near2, total2, small2, hidden, resid, send, recv, own_sem,
):
    net = Net(send, recv)
    net.barrier()

    def kv_slot(index, half):
        if half is None:
            return kv_all.at[pl.ds(index * 16, 16)]
        return kv_all.at[pl.ds(index * 16 + half * 8, 8)]

    keys = ColumnGather(net, kv, kv_slot, own_sem.at[0], 16)
    outw = ColumnGather(net, wo, half_rows(wo_all, 256), own_sem.at[1], 256)
    gate = ColumnGather(net, wg, half_rows(wg_all, GROUP), own_sem.at[2], GROUP)
    up = ColumnGather(net, wu, half_rows(wu_all, GROUP), own_sem.at[3], GROUP)
    down = ColumnGather(net, wd, half_rows(wd_all, HIDDEN), own_sem.at[4], HIDDEN)
    keys.start()
    keys.start_local()
    outw.start()
    outw.start_local()
    keys.relay()
    outw.relay()
    gate.start()
    up.start()
    gate.start_local()
    up.start_local()
    down.start_local()
    keys.forward()
    keys.wait()

    first_key = net.g * GROUP
    query_index = first_key + lax.broadcasted_iota(jnp.int32, (GROUP, GROUP), 0)
    lane = lax.broadcasted_iota(jnp.int32, (GROUP, GROUP), 1)
    query_begin = begin[...]
    scale = HEAD ** (-0.5)
    for head in range(2):
        query = q[:, head * HEAD:(head + 1) * HEAD]

        def body(group, state):
            top, weight, mixed = state
            at = pl.ds(group * 16, 16)
            key = kv_all[at, :, 0:HEAD].reshape(GROUP, HEAD)
            value = kv_all[at, :, HEAD:2 * HEAD].reshape(GROUP, HEAD)
            scores = lax.dot_general(
                query, key, (((1,), (1,)), ((), ())), preferred_element_type=F32
            ) * scale
            index = lane + group * GROUP
            allowed = (index >= query_begin) & (index <= query_index)
            scores = jnp.where(allowed, scores, MASKED)
            newest = jnp.maximum(top, jnp.max(scores, axis=1, keepdims=True))
            weights = jnp.where(allowed, jnp.exp(scores - newest), 0.0)
            shrink = jnp.exp(top - newest)
            return (
                newest,
                weight * shrink + jnp.sum(weights, axis=1, keepdims=True),
                mixed * shrink + dot(weights.astype(BF16), value),
            )

        state = (
            jnp.full((GROUP, 1), MASKED, F32),
            jnp.zeros((GROUP, 1), F32),
            jnp.zeros((GROUP, HEAD), F32),
        )
        top, weight, mixed = lax.fori_loop(0, net.g + 1, body, state)
        hidden[:, head * HEAD:(head + 1) * HEAD] = (mixed / weight).astype(BF16)

    outw.forward()
    outw.wait()
    scatter = PlaneScatter(net, part, near, None, total, small)
    attended = hidden[:, 0:2 * HEAD]
    for h, q_at in QUARTERS:
        for e in range(2):
            k = (h * 2 + q_at) * 2 + e
            part[:, :, :, k * GROUP:(k + 1) * GROUP] = (
                dot(attended, wo_all[k]).astype(BF16).reshape(4, 4, LOCAL, GROUP)
            )
        scatter.step1(h, q_at)
    low = lax.rem(net.y, 2) == 0
    for s in range(16):
        page = kv_all[inv[s]].astype(F32)
        for e in range(2):
            both = page[:, e * HEAD:(e + 1) * HEAD]
            mine = jnp.where(low, both, pltpu.roll(both, HEAD // 2, 1))
            cache[s, e] = mine[:, 0:HEAD // 2].astype(BF16)
    for h, q_at in QUARTERS:
        scatter.step2(h, q_at)
    gate.relay()
    for h, q_at in QUARTERS:
        scatter.step3(h, q_at)
    for h, q_at in QUARTERS:
        scatter.step4(h, q_at)
    for h, q_at in QUARTERS:
        at = pl.ds((h * 2 + q_at) * QUARTER, QUARTER)
        share = scatter.step5(h, q_at)
        resid[:, at] = (tokens[:, at].astype(F32) + share).astype(BF16)
    x_all[net.h] = rms(resid[...].astype(F32), gain[...].astype(F32)).astype(BF16)
    gather = PlaneGather(net, x_all)
    gather.start()
    up.relay()
    down.start()
    gather.step1()
    gather.step2()
    gather.step3()
    gate.forward()
    gather.step4()
    gather.step5()
    gather.step6()
    gate.wait()
    up.forward()
    up.wait()

    @pl.loop(0, 2)
    def _(r):
        gates = jnp.zeros((256, HIDDEN), F32)
        ups = jnp.zeros((256, HIDDEN), F32)
        for k in range(8):
            rows = x_all[pl.ds(r * 8, 8), :, k * GROUP:(k + 1) * GROUP].reshape(256, GROUP)
            gates = gates + dot(rows, wg_all[k])
            ups = ups + dot(rows, wu_all[k])
        hidden[pl.ds(r * 256, 256), :] = (gates / (1.0 + jnp.exp(-gates)) * ups).astype(BF16)

    down.relay()
    down.forward()
    down.wait()
    net.finish()
    scatter = PlaneScatter(net, part, near2, None, total2, small2)
    for h, q_at in QUARTERS:
        for e in range(2):
            k = (h * 2 + q_at) * 2 + e
            part[:, :, :, k * GROUP:(k + 1) * GROUP] = (
                dot(hidden[...], wd_all[k]).astype(BF16).reshape(4, 4, LOCAL, GROUP)
            )
        scatter.step1(h, q_at)
    for h, q_at in QUARTERS:
        scatter.step2(h, q_at)
    for h, q_at in QUARTERS:
        scatter.step3(h, q_at)
    for h, q_at in QUARTERS:
        scatter.step4(h, q_at)
    for h, q_at in QUARTERS:
        at = pl.ds((h * 2 + q_at) * QUARTER, QUARTER)
        out[:, at] = (resid[:, at].astype(F32) + scatter.step5(h, q_at)).astype(BF16)
    net.finish()


def back(inv, q, kv, begin, tokens, gain, wo, wg, wu, wd):
    return pl.pallas_call(
        back_kernel,
        out_shape=(
            jax.ShapeDtypeStruct((LOCAL, WIDTH), BF16),
            jax.ShapeDtypeStruct((16, 2, PAGE, HEAD // 2), BF16),
        ),
        in_specs=[pl.BlockSpec(memory_space=pltpu.SMEM), vmem(), anywhere()]
        + [vmem()] * 3
        + [anywhere()] * 4,
        out_specs=(vmem(), vmem()),
        scratch_shapes=[
            pltpu.VMEM((128, PAGE, 2 * HEAD), BF16),
            pltpu.VMEM((8, 256, GROUP), BF16),
            pltpu.VMEM((8, GROUP, HIDDEN), BF16),
            pltpu.VMEM((8, GROUP, HIDDEN), BF16),
            pltpu.VMEM((8, HIDDEN, GROUP), BF16),
            pltpu.VMEM((16, LOCAL, WIDTH), BF16),
            pltpu.VMEM((4, 4, LOCAL, WIDTH), BF16),
            pltpu.VMEM((4, 3, 4, LOCAL, QUARTER), BF16),
            pltpu.VMEM((4, 4, LOCAL, QUARTER), BF16),
            pltpu.VMEM((4, 3, LOCAL, QUARTER), BF16),
            pltpu.VMEM((4, 3, 4, LOCAL, QUARTER), BF16),
            pltpu.VMEM((4, 4, LOCAL, QUARTER), BF16),
            pltpu.VMEM((4, 3, LOCAL, QUARTER), BF16),
            pltpu.VMEM((GROUP, HIDDEN), BF16),
            pltpu.VMEM((LOCAL, WIDTH), BF16),
            pltpu.SemaphoreType.DMA((160,)),
            pltpu.SemaphoreType.DMA((160,)),
            pltpu.SemaphoreType.DMA((5,)),
        ],
        compiler_params=pltpu.CompilerParams(
            collective_id=1, has_side_effects=True, vmem_limit_bytes=VMEM_LIMIT
        ),
        name="back",
    )(inv, q, kv, begin, tokens, gain, wo, wg, wu, wd)


def per_device(
    tokens, attn_gain, mlp_gain, w_query, w_key, value_projection,
    w_out, w_gate, w_up, w_down, lengths, page_table,
):
    group_index = lax.axis_index("gx")
    token_index = group_index * GROUP + jnp.arange(GROUP, dtype=jnp.int32)
    ends = jnp.sum(
        jnp.where(jnp.arange(6)[:, None] >= jnp.arange(6)[None, :], lengths[None, :], 0), axis=1
    )
    begin = jnp.max(jnp.where(token_index[:, None] >= ends[None, :], ends[None, :], 0), axis=1)
    position = (token_index - begin).astype(F32)
    lane = jnp.arange(HEAD, dtype=jnp.int32)
    freq = ROPE_BASE ** (-(lane % (HEAD // 2)).astype(F32) * 2.0 / HEAD)
    angle = position[:, None] * freq[None, :]
    cos = jnp.cos(angle)
    sin = jnp.sin(angle) * jnp.where(lane < HEAD // 2, -1.0, 1.0)[None, :]
    wqkv = jnp.concatenate([w_query, w_key, value_projection], axis=1)
    cells = page_table[:, 0] * 16 + page_table[:, 1]
    target = group_index * 16 + jnp.arange(16, dtype=jnp.int32)
    inv = jnp.sum(
        jnp.where(
            cells[None, :] == target[:, None], jnp.arange(128, dtype=jnp.int32)[None, :], 0
        ),
        axis=1,
    )
    q, kv = front(tokens, attn_gain[None, :], cos, sin, wqkv)
    return back(
        inv, q, kv, begin[:, None], tokens, mlp_gain[None, :], w_out, w_gate, w_up, w_down
    )


def solution(mesh):
    placed = (
        P(("gx", "gy"), None),
        P(),
        P(),
        P("gx", "gy"),
        P("gx", "gy"),
        P("gx", "gy"),
        P("gy", "gx"),
        P("gx", "gy"),
        P("gx", "gy"),
        P("gy", "gx"),
        P(),
        P(),
    )
    return jax.shard_map(
        per_device,
        mesh=mesh,
        in_specs=placed,
        out_specs=(P(("gx", "gy"), None), P("gx", None, None, "gy")),
        check_vma=False,
    )
```

time: 551 us -> 201 us (0.36)
  waiting for transfers between devices: 419 us -> 0 us
  Pallas kernels: 0 us -> 189 us
  matrix products: 52.7 us -> 0 us
  blocking collectives: 28.8 us -> 0 us
  other arithmetic: 23.6 us -> 3.58 us
  between operations: 14.8 us -> 0.74 us
  starting transfers between devices: 7.29 us -> 0 us
    all_gather x9 -> x0, waiting for transfers between devices: 263 us -> none  [the longest x1 54.3 us: per_device(): lax.all_gather(rms_scale(residual, mlp_gain).astype(jnp.bfloat16), 'gy',...]
    pallas_call x0 -> x2, Pallas kernels: none -> 189 us  [the longest x1 150 us: back(): pl.pallas_call(back_kernel, out_shape=(jax.ShapeDtypeStruct((LOCAL, WIDTH...]
    reduce_scatter x2 -> x0, waiting for transfers between devices: 140 us -> none  [the longest x1 77.2 us: per_device(): lax.psum_scatter(partial_value.astype(jnp.bfloat16), 'gy', scatter_dimens...]
    dot_general x10 -> x0, matrix products: 52.7 us -> none  [the longest x4 21.2 us: row_products(): jnp.dot(source, piece, preferred_element_type=jnp.float32)]
    all_gather x2 -> x0, blocking collectives: 28.8 us -> none  [the longest x1 14.6 us: per_device(): lax.all_gather(key_weight, 'gx', axis=0, tiled=True)]
    convert_element_type x8 -> x1, other arithmetic: 6.76 us -> 0.01 us  [per_device(): position = (token_index - begin).astype(F32)]
    reduce_sum x7 -> x2, other arithmetic: 7.19 us -> 0.78 us  [the longest x1 0.67 us: per_device(): jnp.sum(jnp.where(cells[None, :] == target[:, None], jnp.arange(128, dtyp...]
    all_to_all x1 -> x0, waiting for transfers between devices: 6.04 us -> none  [per_device(): lax.all_to_all(outgoing, 'gx', split_axis=0, concat_axis=0, tiled=True)]
  transfers between devices with their start and end apart: 14 -> 0, of which waited for: 13 -> 0; matrix products, arithmetic and copies ran while one was open for 10% -> 0% of each run, Pallas kernels for 0% -> 0%
where the time goes in v1:
time: 201 us; the launch traced here: 200 us
  Pallas kernels  189 us (94%)
  local copies, waits for them, and re-layouts  6.76 us (3%)
  other arithmetic  3.58 us (2%)
    pallas_call x1, Pallas kernels, back(): pl.pallas_call(back_kernel, out_shape=(jax.ShapeDtypeStruct((LOCAL, WIDTH...  150 us
    pallas_call x1, Pallas kernels, front(): pl.pallas_call(front_kernel, out_shape=(jax.ShapeDtypeStruct((GROUP, 2 *...  39.5 us
    unnamed x20, local copies, waits for them, and re-layouts  4.68 us

profile of v1, /device:TPU:0, one launch (start us, length us, event | category | flops | bytes accessed | tf_op | source)
XLA Modules:
  0.0 200.3 jit_solution(15257687926864809830)
XLA Ops:
  0.6 0.0 copy-start.7
  0.7 0.6 copy-done.7
  1.3 0.1 select_reduce_fusion.2
  1.4 0.1 select_reduce_fusion
  1.5 0.0 copy-start.2
  1.5 0.0 copy-start.3
  1.5 1.8 fusion
  3.4 0.0 copy-start
  3.4 0.0 copy-done.2
  3.4 0.1 copy.19
  3.5 0.0 copy-done.3
  3.5 0.1 copy.20
  3.6 0.7 copy-done
  4.3 0.0 copy-start.4
  4.3 0.9 pad_maximum_fusion.wqkv
  5.2 0.0 copy-done.4
  5.2 0.6 broadcast_in_dim.63.gain
  5.8 39.5 %front.1 = (bf16[512,256]{1,0:T(8,128)(2,1)}, bf16[16,32,256]{2,1,0:T(8,128)(2,1)}) custom-call(bf16[32,4096]{1,0:T(8,128)(2,1)} %tokens.3, bf16[1,4096]{1,0:T(2,128)(2,1)} %broadcast_in_dim.63.gain, f32[512,128]{1,0:T(8,128)} %get-tuple-element.7.cos, f32[512,128]{1,0:T(8,128)} %get-tuple-element.6.sin, bf16[512,384]{1,0:T(8,128)(2,1)} %pad_maximum_fusion.wqkv), custom_call_target="tpu_custom_call" | custom-call | tf_op jit(solution)/shard_map/front/pallas_call | solution.py:358
  45.3 0.0 copy-start.5
  45.3 0.9 copy.21.begin
  46.2 0.0 copy-start.6
  46.2 0.7 copy-done.6
  46.9 0.7 select_reduce_fusion.1.inv
  47.5 0.0 copy-done.5
  47.5 0.6 broadcast_in_dim.69.gain
  48.1 149.7 %back.1 = (bf16[32,4096]{1,0:T(8,128)(2,1)}, bf16[16,2,32,64]{3,2,1,0:T(8,128)(2,1)}) custom-call(s32[16]{0:T(128)} %select_reduce_fusion.1.inv, bf16[512,256]{1,0:T(8,128)(2,1)} %get-tuple-element.4.q, bf16[16,32,256]{2,1,0:T(8,128)(2,1)} %get-tuple-element.5.kv, s32[512,1]{1,0:T(8,128)} %copy.21.begin, bf16[32,4096]{1,0:T(8,128)(2,1)} %tokens.3, ...), custom_call_target="tpu_custom_call" | custom-call | tf_op jit(solution)/shard_map/back/pallas_call | solution.py:530
  197.9 0.0 copy-start.1
  197.9 1.7 copy.24
  199.6 0.0 copy-done.1
  199.6 0.7 copy.25
  (5 shorter events, 0.0 us)
Async XLA Ops:
  0.6 0.7 copy-start.7
  1.5 1.9 copy-start.2
  1.5 2.0 copy-start.3
  3.4 1.0 copy-start
  4.3 0.9 copy-start.4
  45.3 2.2 %copy-start.5 = (bf16[4096]{0:T(1024)(128)(2,1)S(1)}, bf16[4096]{0:T(1024)(128)(2,1)}, u32[]{:S(2)}) copy-start(bf16[4096]{0:T(1024)(128)(2,1)} %param.14) | copy-start | bytes 24580
  46.2 0.7 copy-start.6
  197.9 1.7 copy-start.1
